TPU v7x, 256 devices: a whole 4x4x8 slice. The times are simulated.
256 devices in a mesh: row: 16 (over y, x), col: 8 (over z_lo, core), band: 2 (over z_hi).
Axes of the slice: x: 4, y: 4, z: 8 (z_hi: 2, z_lo: 4; z = z_hi * 4 + z_lo), core: 2. Of those that a mesh axis runs over, the one named last changes fastest.
Arguments:
- panel: bfloat16 [32, 512, 512], P('row', ('col', 'band')), may hold values from -6 to 6
- inverse: bfloat16 [2, 512, 512], replicated, may hold values from -0.25 to 0.25
- trail_grad: bfloat16 [32, 32, 512, 512], P('row', ('col', 'band')), may hold values from -0.046875 to 0.046875
- factor_grad: bfloat16 [32, 512, 512], P('row', ('col', 'band')), may hold values from -6 to 6
- present: int32 [32, 32], P('row', ('col', 'band')), may hold values from 0 to 1, as said below
- supernode: int32 [32], replicated, may hold values from 0 to 1
Outputs:
- panel_adjoint: bfloat16 [32, 512, 512], P('row', ('col', 'band'))
- inverse_adjoint: float32 [2, 512, 512], replicated
Inputs may be any that keep to these rules, and one draw needn't show every extreme that they name: Every diagonal tile is present; rows differ widely in how many tiles are present.
All inputs are finite; a program needn't handle non-finite values.
Results may differ from a plain program's by a relative error of at most 0.0055.
Values may be sent and summed in bfloat16 or wider, within the bound.
A program may use at most 64 MiB of HBM per device.

v0:
```python
import jax
import jax.numpy as jnp
from jax import lax
from jax.sharding import PartitionSpec as P


def from_root(value, axis, source):
    kept = jnp.where(lax.axis_index(axis) == source, value, 0).astype(value.dtype)
    return lax.psum(kept, axis)


def pick_inverse(inverse, labels):
    first = inverse[0][None, :, :]
    second = inverse[1][None, :, :]
    return jnp.where((labels == 0)[:, None, None], first, second)


def local(panel, inverse, trail_grad, factor_grad, present, supernode):
    rows_here = trail_grad.shape[0]
    cols_here = trail_grad.shape[1]
    tile = trail_grad.shape[2]
    total_rows = rows_here * lax.axis_size("row")
    row_index = lax.axis_index("row")
    col_index = lax.axis_index(("col", "band"))
    row_labels = lax.dynamic_slice_in_dim(supernode, row_index * rows_here, rows_here)
    col_labels = lax.dynamic_slice_in_dim(supernode, col_index * cols_here, cols_here)
    root = col_index * cols_here // rows_here
    row_inverse = pick_inverse(inverse, row_labels)
    factor_piece = jnp.einsum(
        "iab,ibc->iac", panel, row_inverse, preferred_element_type=jnp.float32
    ).astype(jnp.bfloat16)
    factor_row = lax.all_gather(factor_piece, ("col", "band"), axis=1, tiled=True)
    factor_block = from_root(factor_row, "row", root)
    weight = present * (row_labels[:, None] == col_labels[None, :]).astype(jnp.int32)
    masked = trail_grad * weight.astype(jnp.bfloat16)[:, :, None, None]
    mirror_part = jnp.einsum(
        "ijab,iae->jbe", masked, factor_row, preferred_element_type=jnp.float32
    )
    mirror = lax.psum(mirror_part, "row")
    mirror_cols = jnp.transpose(mirror, (1, 0, 2))
    is_owner = (row_index == root).astype(jnp.float32)
    placed = mirror_cols
    placed = placed * is_owner
    direct = jnp.einsum("ijab,jbe->aie", masked, factor_block, preferred_element_type=jnp.float32)
    summed = lax.psum_scatter(direct + placed, ("col", "band"), scatter_dimension=0, tiled=True)
    factor_total = (jnp.transpose(factor_grad.astype(jnp.float32), (1, 0, 2)) - summed).astype(
        jnp.bfloat16
    )
    panel_adjoint = jnp.einsum(
        "aie,ife->iaf", factor_total, row_inverse, preferred_element_type=jnp.float32
    ).astype(jnp.bfloat16)
    onehot = (row_labels[:, None] == jnp.arange(2, dtype=jnp.int32)[None, :]).astype(jnp.float32)
    terms = jnp.einsum("iaf,aie->ife", panel, factor_total, preferred_element_type=jnp.float32)
    local_grad = jnp.einsum("is,ife->sfe", onehot, terms)
    inverse_adjoint = lax.psum(local_grad, ("row", "col", "band")) / jnp.sqrt(
        jnp.float32(total_rows * tile)
    )
    return (panel_adjoint, inverse_adjoint)


def solution(mesh):
    in_specs = (
        P("row", ("col", "band"), None),
        P(),
        P("row", ("col", "band"), None, None),
        P("row", ("col", "band"), None),
        P("row", ("col", "band")),
        P(),
    )
    out_specs = (P("row", ("col", "band"), None), P())
    return jax.shard_map(local, mesh=mesh, in_specs=in_specs, out_specs=out_specs, check_vma=False)
```

profile of v0, /device:TPU:1, one launch (start us, length us, event | category | flops | bytes accessed | tf_op | source)
XLA Modules:
  0.0 710.4 jit_solution(867655354191725240)
XLA Ops:
  7.2 0.0 copy-start
  7.2 0.0 copy-start.4
  7.2 0.0 all-gather.2.cloned.1.call-start
  7.2 1.3 slice_bitcast_fusion.1
  8.5 0.0 copy-done.4
  8.5 0.1 broadcast_compare_fusion
  8.6 0.0 copy-done
  8.6 0.0 copy-start.3
  8.6 1.1 fusion.19
  9.7 0.0 all-gather.2.cloned.1.call-update
  9.7 0.0 all-reduce.6.cloned.1.call-start
  9.8 91.9 %all-gather.2.cloned.1.call-done = bf16[2,512,512]{2,1,0:T(8,128)(2,1)} async-done(((bf16[2,32,512]{2,1,0:T(8,128)(2,1)}), bf16[2,512,512]{2,1,0:T(8,128)(2,1)}) %all-gather.2.cloned.1.call-update) | async-done | bytes 1048592 | tf_op jit(solution)/shard_map/all_gather | solution.py:32
  101.7 0.0 copy-start.1
  101.7 1.1 broadcast_select_fusion
  102.7 0.0 all-reduce.6.cloned.1.call-update
  102.8 0.0 all-reduce.8.cloned.1.call-start
  102.8 0.1 dynamic_slice.7
  102.9 0.0 copy-done.3
  102.9 0.1 fusion.36
  103.0 0.3 copy-done.1
  103.3 4.2 fusion.4
  107.5 0.0 all-reduce.8.cloned.1.call-update
  107.5 0.0 all-reduce.12.cloned.1.call-start
  107.6 96.3 %all-reduce.6.cloned.1.call-done = bf16[2,512,512]{2,1,0:T(8,128)(2,1)} async-done(((bf16[2,512,512]{2,1,0:T(8,128)(2,1)}), bf16[2,512,512]{2,1,0:T(8,128)(2,1)}) %all-reduce.6.cloned.1.call-update) | async-done | bytes 1048592 | tf_op jit(solution)/shard_map/psum | solution.py:9
  203.9 104.6 %all-reduce.8.cloned.1.call-done = f32[2,512,512]{1,2,0:T(8,128)} async-done(((f32[2,512,512]{1,2,0:T(8,128)}), f32[2,512,512]{1,2,0:T(8,128)}) %all-reduce.8.cloned.1.call-update) | async-done | bytes 2097168 | tf_op jit(solution)/shard_map/psum | solution.py:39
  308.5 3.9 bitcast_add_fusion
  312.5 2.4 copy.26
  314.9 0.0 copy-start.5
  314.9 0.0 copy-start.2
  314.9 0.0 all-reduce.12.cloned.1.call-update
  314.9 0.0 all-reduce.10.cloned.1.call-start
  315.0 0.6 copy-done.5
  315.6 0.6 dynamic-slice
  316.8 114.4 %all-reduce.12.cloned.1.call-done = f32[512,2,512]{2,1,0:T(2,128)} async-done(((f32[512,2,512]{2,1,0:T(2,128)}), f32[512,2,512]{2,1,0:T(2,128)}) %all-reduce.12.cloned.1.call-update) | async-done | bytes 2097168
  431.2 0.9 constant_dynamic-slice_fusion
  432.1 0.0 copy-done.2
  432.1 0.5 convolution_bitcast_fusion
  432.6 1.0 copy.29
  433.6 2.8 fusion.33
  436.4 0.0 all-reduce.10.cloned.1.call-update
  436.4 1.1 fusion.16
  437.6 262.1 %all-reduce.10.cloned.1.call-done = f32[2,512,512]{2,0,1:T(2,128)} async-done(((f32[2,512,512]{2,0,1:T(2,128)}), f32[2,512,512]{2,0,1:T(2,128)}) %all-reduce.10.cloned.1.call-update) | async-done | bytes 2097168 | tf_op jit(solution)/shard_map/psum | solution.py:55
  699.7 2.5 broadcast_multiply_fusion
  702.2 1.7 copy.30
Async XLA Ops:
  7.2 1.4 copy-start
  7.2 1.3 copy-start.4
  7.2 94.5 %all-gather.2.cloned.1.call-start = ((), (), s32[]{:S(2)}) async-start(), calls=%async_computation | async-start | bytes 1114112 | tf_op jit(solution)/shard_map/all_gather | solution.py:32
  8.6 94.3 %copy-start.3 = (s32[2,2]{1,0:T(2,128)S(1)}, s32[2,2]{1,0:T(2,128)}, u32[]{:S(2)}) copy-start(s32[2,2]{1,0:T(2,128)} %param.10) | copy-start | bytes 52
  9.7 194.2 %all-reduce.6.cloned.1.call-start = ((), (), s32[]{:S(2)}) async-start(), calls=%async_computation.1 | async-start | bytes 2097152 | tf_op jit(solution)/shard_map/psum | solution.py:9
  101.7 1.6 copy-start.1
  102.8 205.8 %all-reduce.8.cloned.1.call-start = ((), (), s32[]{:S(2)}) async-start(), calls=%async_computation.2 | async-start | bytes 4194304 | tf_op jit(solution)/shard_map/psum | solution.py:39
  107.5 323.6 %all-reduce.12.cloned.1.call-start = ((), (), s32[]{:S(2)}) async-start(), calls=%async_computation.4 | async-start | bytes 4194304
  314.9 0.7 copy-start.5
  314.9 117.2 %copy-start.2 = (bf16[2,32,512]{2,1,0:T(8,128)(2,1)S(1)}, bf16[2,32,512]{2,1,0:T(8,128)(2,1)}, u32[]{:S(2)}) copy-start(bf16[2,32,512]{2,1,0:T(8,128)(2,1)} %param.9) | copy-start | bytes 196612
  314.9 384.7 %all-reduce.10.cloned.1.call-start = ((), (), s32[]{:S(2)}) async-start(), calls=%async_computation.3 | async-start | bytes 4194304 | tf_op jit(solution)/shard_map/psum | solution.py:55
Sparse Core Ops, SparseCore 0:
  10.4 91.2 all-gather.1
  104.9 98.9 all-reduce.5
  207.8 100.6 all-reduce.7
  315.0 116.0 all-reduce.11
  437.0 262.6 all-reduce.9
where the time goes:
time: 711 us; the launch traced here: 710 us
  waiting for transfers between devices  669 us (94%)
  between operations  14.5 us (2%)
  matrix products  13.7 us (2%)
  local copies, waits for them, and re-layouts  8.87 us (1%)
    psum x1, waiting for transfers between devices, local(): lax.psum(local_grad, ('row', 'col', 'band'))  262 us
    unnamed x6, waiting for transfers between devices  114 us
    psum x1, waiting for transfers between devices, local(): mirror = lax.psum(mirror_part, 'row')  105 us
    psum x1, waiting for transfers between devices, from_root(): return lax.psum(kept, axis)  96.3 us
    all_gather x1, waiting for transfers between devices, local(): lax.all_gather(factor_piece, ('col', 'band'), axis=1, tiled=True)  91.9 us
  transfers between devices with their start and end apart: 5, of which 5 were waited for; matrix products, arithmetic and copies ran while one was open for 1% of the time, Pallas kernels for 0%

commit v1 on v0

v1 whole, which is shorter than its diff:
```python
import jax
import jax.numpy as jnp
from jax import lax
from jax.experimental import pallas as pl
from jax.experimental.pallas import tpu as pltpu
from jax.sharding import PartitionSpec as P

MESH = pl.DeviceIdType.MESH
F32 = jnp.float32
BF16 = jnp.bfloat16
N = 16
ZN = 8
R = 32
TILE = 512


def rem(a, b):
    return lax.rem(a, jnp.int32(b))


def div(a, b):
    return lax.div(a, jnp.int32(b))


def loop(lo, hi, body):
    def step(i, carry):
        body(i)
        return carry

    lax.fori_loop(lo, hi, step, 0)


def kernel(
    panel, inverse, trail_hbm, factor_grad, present, supernode,
    adjoint, inv_out,
    tm, tt, frow, pg, fcol, dpart, dsib, dsum, drecv, dtot, mpart, mrecv, mred, mfin,
    tslice, trecv, rpart, rrecv, gz, gx,
    t_sem, fz_s, fz_r, pz_s, pz_r, perm_s, perm_r, fx_s, fx_r,
    ds_s, ds_r, dz_s, dz_r, mx_s, mx_r, mp_s, mp_r, tz_s, tz_r, rx_s, rx_r, gz_s, gz_r, gx_s, gx_r,
):
    r = lax.axis_index("row")
    col = lax.axis_index("col")
    band = lax.axis_index("band")
    core = rem(col, 2)
    z = band * 4 + div(col, 2)
    c = col * 2 + band
    sib_col = col + 1 - 2 * core

    def z_dev(k):
        return (r, div(k, 2), rem(k, 2))

    def x_dev(p):
        return (p, col, band)

    def index_at(zz, cc):
        return rem(zz, 4) * 4 + cc * 2 + div(zz, 4)

    def ring(d):
        half = div(d + 1, 2)
        return rem(z + ZN + half * (2 * rem(d, 2) - 1), ZN)

    sib = (r, sib_col, band)
    turned = (c, div(r, 2), rem(r, 2))

    def remote(src, dst, ss, rs, dev):
        return pltpu.make_async_remote_copy(
            src_ref=src, dst_ref=dst, send_sem=ss, recv_sem=rs, device_id=dev, device_id_type=MESH
        )

    trail_copy = pltpu.make_async_copy(trail_hbm, tm, t_sem)
    trail_copy.start()

    barrier = pltpu.get_barrier_semaphore()

    def greet(d):
        pl.semaphore_signal(barrier, inc=1, device_id=z_dev(rem(c + d, N)), device_id_type=MESH)
        pl.semaphore_signal(barrier, inc=1, device_id=x_dev(rem(r + d, N)), device_id_type=MESH)

    loop(1, N, greet)

    @pl.when(r != c)
    def _():
        pl.semaphore_signal(barrier, inc=1, device_id=turned, device_id_type=MESH)

    s_row = [supernode[2 * r + i] for i in range(2)]
    s_col = [supernode[2 * c + j] for j in range(2)]

    mine = panel[...].reshape(2 * R, TILE)
    y0 = jnp.dot(mine, inverse[0], preferred_element_type=F32)
    y1 = jnp.dot(mine, inverse[1], preferred_element_type=F32)
    row_tile = lax.broadcasted_iota(jnp.int32, (2 * R, TILE), 0) // R
    row_super = jnp.where(row_tile == 0, s_row[0], s_row[1])
    piece = jnp.where(row_super == 0, y0, y1).astype(BF16)
    frow[c] = piece
    pg[c] = mine

    @pl.when(r == c)
    def _():
        fcol[r] = piece

    @pl.when(r == c)
    def _():
        pl.semaphore_wait(barrier, 2 * (N - 1))

    @pl.when(r != c)
    def _():
        pl.semaphore_wait(barrier, 2 * (N - 1) + 1)
        remote(frow.at[c], fcol.at[c], perm_s, perm_r, turned).start()

    def gather_z_start(buf, ss, rs):
        def send(d):
            k = index_at(ring(d), core)
            remote(buf.at[c], buf.at[c], ss.at[d], rs.at[c], z_dev(k)).start()

        loop(1, ZN, send)
        remote(buf.at[c], buf.at[c], ss.at[0], rs.at[c], sib).start()

    def gather_z_pass(buf, ss, rs):
        def forward(d):
            k = index_at(ring(d), core)
            copy = remote(buf.at[k], buf.at[k], ss.at[ZN - 1 + d], rs.at[k], sib)
            copy.wait_recv()
            copy.start()

        loop(1, ZN, forward)

    def gather_z_end(buf, ss, rs):
        def finish(d):
            k = index_at(rem(z + d, ZN), 1 - core)
            remote(buf.at[k], buf.at[k], ss.at[d], rs.at[k], sib).wait_recv()

        loop(0, ZN, finish)

        def drain(d):
            remote(buf.at[c], buf.at[c], ss.at[d], rs.at[c], sib).wait_send()

        loop(0, 2 * ZN - 1, drain)

    gather_z_start(frow, fz_s, fz_r)
    gather_z_start(pg, pz_s, pz_r)

    trail_copy.wait()
    for i in range(2):
        for j in range(2):
            weight = present[i, j] * (s_row[i] == s_col[j]).astype(jnp.int32)
            kept = tm[i, j].astype(F32) * weight.astype(F32)
            tm[i, j] = kept.astype(BF16)
            tt[i, j] = kept.T.astype(BF16)

    @pl.when(r != c)
    def _():
        remote(frow.at[c], fcol.at[r], perm_s, perm_r, turned).wait_recv()

    def gather_x(d):
        remote(fcol.at[r], fcol.at[r], fx_s.at[d], fx_r.at[r], x_dev(rem(r + d, N))).start()

    loop(1, N, gather_x)

    gather_z_pass(frow, fz_s, fz_r)
    gather_z_end(frow, fz_s, fz_r)

    for j in range(2):
        total = jnp.zeros((TILE, TILE), F32)
        for i in range(2):
            rows = frow[:, i * R:(i + 1) * R, :].reshape(TILE, TILE)
            total = total + jnp.dot(tt[i, j], rows, preferred_element_type=F32)
        mpart[:, j * R:(j + 1) * R, :] = total.astype(BF16).reshape(N, R, TILE)

    def scatter_x(d):
        p = rem(r + d, N)
        remote(mpart.at[p], mrecv.at[r], mx_s.at[d], mx_r.at[r], x_dev(p)).start()

    loop(1, N, scatter_x)

    gather_z_pass(pg, pz_s, pz_r)

    def wait_x(d):
        p = rem(r + d, N)
        remote(fcol.at[p], fcol.at[p], fx_s.at[d], fx_r.at[p], x_dev(p)).wait_recv()

    loop(1, N, wait_x)

    for i in range(2):
        total = jnp.zeros((TILE, TILE), F32)
        for j in range(2):
            rows = fcol[:, j * R:(j + 1) * R, :].reshape(TILE, TILE)
            total = total + jnp.dot(tm[i, j], rows, preferred_element_type=F32)
        dpart[:, i * R:(i + 1) * R, :] = total.astype(BF16).reshape(N, R, TILE)

    def to_sibling(d):
        k = index_at(ring(ZN - 1 - d), 1 - core)
        remote(dpart.at[k], dsib.at[k], ds_s.at[d], ds_r.at[k], sib).start()

    loop(0, ZN, to_sibling)

    def pair_sum(d):
        k = index_at(ring(ZN - 1 - d), core)
        remote(dsib.at[k], dsib.at[k], ds_s.at[d], ds_r.at[k], sib).wait_recv()
        dsum[k] = (dpart[k].astype(F32) + dsib[k].astype(F32)).astype(BF16)
        remote(dsum.at[k], drecv.at[c], dz_s.at[d], dz_r.at[c], z_dev(k)).start()

    loop(0, ZN - 1, pair_sum)
    remote(dsib.at[c], dsib.at[c], ds_s.at[0], ds_r.at[c], sib).wait_recv()
    dtot[...] = dpart[c].astype(F32) + dsib[c].astype(F32)

    mred[...] = mpart[r].astype(F32)

    def mirror_sum(d):
        p = rem(r + d, N)
        remote(mrecv.at[p], mrecv.at[p], mx_s.at[d], mx_r.at[p], x_dev(p)).wait_recv()
        mred[...] = mred[...] + mrecv[p].astype(F32)

    loop(1, N, mirror_sum)
    mfin[0] = mred[...].astype(BF16)

    @pl.when(r == c)
    def _():
        mfin[1] = mred[...].astype(BF16)

    @pl.when(r != c)
    def _():
        remote(mfin.at[0], mfin.at[1], mp_s, mp_r, turned).start()

    def direct_sum(d):
        k = index_at(ring(d), core)
        remote(drecv.at[k], drecv.at[k], dz_s.at[d], dz_r.at[k], z_dev(k)).wait_recv()
        dtot[...] = dtot[...] + drecv[k].astype(F32)

    loop(1, ZN, direct_sum)
    gather_z_end(pg, pz_s, pz_r)

    @pl.when(r != c)
    def _():
        remote(mfin.at[0], mfin.at[1], mp_s, mp_r, turned).wait_recv()

    grad = factor_grad[...].reshape(2 * R, TILE).astype(F32)
    rounded = (grad - dtot[...] - mfin[1].astype(F32)).astype(BF16)
    wide = rounded.astype(F32)

    none = jnp.zeros_like(wide)
    odd = rem(c, 2)
    padded = jnp.concatenate(
        [jnp.where(odd == 0, wide, none), jnp.where(odd == 0, none, wide)], axis=0
    )
    tslice[...] = padded.T.astype(BF16).reshape(N, R, 128)
    trecv[c] = tslice[c]

    def spread(d):
        k = rem(c + d, N)
        remote(tslice.at[k], trecv.at[c], tz_s.at[d], tz_r.at[c], z_dev(k)).start()

    loop(1, N, spread)

    dims = (((1,), (1,)), ((), ()))
    y0 = lax.dot_general(rounded, inverse[0], dims, preferred_element_type=F32)
    y1 = lax.dot_general(rounded, inverse[1], dims, preferred_element_type=F32)
    adjoint[...] = jnp.where(row_super == 0, y0, y1).astype(BF16).reshape(2, R, TILE)

    def wait_slice(d):
        k = rem(c + d, N)
        remote(trecv.at[k], trecv.at[k], tz_s.at[d], tz_r.at[k], z_dev(k)).wait_recv()

    loop(1, N, wait_slice)

    lane_tile = rem(lax.broadcasted_iota(jnp.int32, (R, 128), 1), 2 * R) // R
    lane_super = jnp.where(lane_tile == 0, s_row[0], s_row[1])
    blocks = []
    for q in range(N // 2):
        both = trecv[2 * q].astype(F32) + trecv[2 * q + 1].astype(F32)
        zero = jnp.zeros_like(both)
        blocks.append(
            jnp.concatenate(
                [jnp.where(lane_super == 0, both, zero), jnp.where(lane_super == 0, zero, both)], axis=0
            ).astype(BF16)
        )
    left = jnp.concatenate(blocks, axis=1)
    slab = jnp.dot(left, pg[...].reshape(2 * TILE, TILE), preferred_element_type=F32)
    for p in range(N):
        g, h = p // 2, p % 2
        rpart[p] = slab[8 * g:8 * g + 8, 256 * h:256 * h + 256]

    def reduce_x(d):
        p = rem(r + d, N)
        remote(rpart.at[p], rrecv.at[r], rx_s.at[d], rx_r.at[r], x_dev(p)).start()

    loop(1, N, reduce_x)
    rrecv[r] = rpart[r]

    def wait_reduce(d):
        p = rem(r + d, N)
        remote(rrecv.at[p], rrecv.at[p], rx_s.at[d], rx_r.at[p], x_dev(p)).wait_recv()

    loop(1, N, wait_reduce)
    done = rrecv[0]
    for p in range(1, N):
        done = done + rrecv[p]
    gz[c] = done * (1.0 / 128.0)

    half = div(c, ZN)

    def collect(d):
        k = index_at(rem(z + d, ZN), half)

        @pl.when(k != c)
        def _():
            remote(gz.at[c], gz.at[c], gz_s.at[d], gz_r.at[c], z_dev(k)).start()

    loop(0, ZN, collect)

    def wait_collect(d):
        k = core * ZN + d

        @pl.when(k != c)
        def _():
            remote(gz.at[k], gz.at[k], gz_s.at[d], gz_r.at[k], z_dev(k)).wait_recv()

    loop(0, ZN, wait_collect)
    own = gz[pl.ds(core * ZN, ZN)].reshape(8 * ZN, 256).astype(BF16)
    gx[r, core] = own

    def spread_x(d):
        remote(gx.at[r, core], gx.at[r, core], gx_s.at[d], gx_r.at[r, core], x_dev(rem(r + d, N))).start()

    loop(1, N, spread_x)
    remote(gx.at[r, core], gx.at[r, core], gx_s.at[0], gx_r.at[r, core], sib).start()

    def pass_x(d):
        p = rem(r + N - d, N)
        copy = remote(gx.at[p, core], gx.at[p, core], gx_s.at[N - 1 + d], gx_r.at[p, core], sib)
        copy.wait_recv()
        copy.start()

    loop(1, N, pass_x)

    def wait_pass(d):
        p = rem(r + N - d, N)
        remote(gx.at[p, 1 - core], gx.at[p, 1 - core], gx_s.at[0], gx_r.at[p, 1 - core], sib).wait_recv()

    loop(0, N, wait_pass)

    for p in range(N):
        g, h = p // 2, p % 2
        for a in range(2):
            inv_out[g // 4, a * ZN:(a + 1) * ZN, g % 4, :, 256 * h:256 * h + 256] = (
                gx[p, a].astype(F32).reshape(ZN, 8, 256)
            )

    @pl.when(r != c)
    def _():
        remote(frow.at[c], fcol.at[r], perm_s, perm_r, turned).wait_send()
        remote(mfin.at[0], mfin.at[1], mp_s, mp_r, turned).wait_send()

    def drain_x(d):
        remote(fcol.at[r], fcol.at[r], fx_s.at[d], fx_r.at[r], sib).wait_send()
        remote(mpart.at[r], mrecv.at[r], mx_s.at[d], mx_r.at[r], sib).wait_send()
        remote(tslice.at[c], trecv.at[c], tz_s.at[d], tz_r.at[c], sib).wait_send()
        remote(rpart.at[r], rrecv.at[r], rx_s.at[d], rx_r.at[r], sib).wait_send()

    loop(1, N, drain_x)

    def drain_z(d):
        remote(dpart.at[c], dsib.at[c], ds_s.at[d], ds_r.at[c], sib).wait_send()

        @pl.when(d < ZN - 1)
        def _():
            remote(dsum.at[c], drecv.at[c], dz_s.at[d], dz_r.at[c], sib).wait_send()

        @pl.when(index_at(rem(z + d, ZN), half) != c)
        def _():
            remote(gz.at[c], gz.at[c], gz_s.at[d], gz_r.at[c], sib).wait_send()

    loop(0, ZN, drain_z)

    def drain_g(d):
        remote(gx.at[r, core], gx.at[r, core], gx_s.at[d], gx_r.at[r, core], sib).wait_send()

    loop(0, 2 * N - 1, drain_g)


def local(panel, inverse, trail_grad, factor_grad, present, supernode):
    vmem = pl.BlockSpec(memory_space=pltpu.VMEM)
    smem = pl.BlockSpec(memory_space=pltpu.SMEM)
    dma = pltpu.SemaphoreType.DMA
    pieces = pltpu.VMEM((N, 2 * R, TILE), BF16)
    adjoint, spread = pl.pallas_call(
        kernel,
        out_shape=(
            jax.ShapeDtypeStruct((2, R, TILE), BF16),
            jax.ShapeDtypeStruct((2, N, 4, 8, TILE), F32),
        ),
        in_specs=[vmem, vmem, pl.BlockSpec(memory_space=pl.ANY), vmem, smem, smem],
        out_specs=(vmem, vmem),
        scratch_shapes=[
            pltpu.VMEM((2, 2, TILE, TILE), BF16),
            pltpu.VMEM((2, 2, TILE, TILE), BF16),
            pieces, pieces, pieces,
            pieces, pieces, pieces, pieces,
            pltpu.VMEM((2 * R, TILE), F32),
            pieces, pieces,
            pltpu.VMEM((2 * R, TILE), F32),
            pltpu.VMEM((2, 2 * R, TILE), BF16),
            pltpu.VMEM((N, R, 128), BF16),
            pltpu.VMEM((N, R, 128), BF16),
            pltpu.VMEM((N, 8, 256), F32),
            pltpu.VMEM((N, 8, 256), F32),
            pltpu.VMEM((N, 8, 256), F32),
            pltpu.VMEM((N, 2, 64, 256), BF16),
            dma,
            dma((15,)), dma((N,)), dma((15,)), dma((N,)),
            dma, dma,
            dma((N,)), dma((N,)),
            dma((ZN,)), dma((N,)), dma((ZN,)), dma((N,)),
            dma((N,)), dma((N,)),
            dma, dma,
            dma((N,)), dma((N,)),
            dma((N,)), dma((N,)),
            dma((ZN,)), dma((N,)),
            dma((31,)), dma((N, 2)),
        ],
        compiler_params=pltpu.CompilerParams(collective_id=0, has_side_effects=True),
    )(panel, inverse, trail_grad, factor_grad, present, supernode)
    inverse_adjoint = jnp.swapaxes(spread.reshape(2, TILE, TILE), 1, 2)
    return adjoint, inverse_adjoint


def solution(mesh):
    assert dict(mesh.shape) == {"row": N, "col": 8, "band": 2}
    in_specs = (
        P("row", ("col", "band"), None),
        P(),
        P("row", ("col", "band"), None, None),
        P("row", ("col", "band"), None),
        P("row", ("col", "band")),
        P(),
    )
    out_specs = (P("row", ("col", "band"), None), P())
    return jax.shard_map(local, mesh=mesh, in_specs=in_specs, out_specs=out_specs, check_vma=False)
```

time: 711 us -> 95.9 us (0.13)
  waiting for transfers between devices: 669 us -> 0 us
  Pallas kernels: 0 us -> 91.6 us
  between operations: 14.5 us -> 0.65 us
  matrix products: 13.7 us -> 0 us
    psum x3 -> x0, waiting for transfers between devices: 463 us -> none  [the longest x1 262 us: local(): lax.psum(local_grad, ('row', 'col', 'band'))]
    unnamed x6 -> x0, waiting for transfers between devices: 114 us -> none
    all_gather x1 -> x0, waiting for transfers between devices: 91.9 us -> none  [local(): lax.all_gather(factor_piece, ('col', 'band'), axis=1, tiled=True)]
    pallas_call x0 -> x1, Pallas kernels: none -> 91.6 us  [local(): pl.pallas_call(kernel, out_shape=(jax.ShapeDtypeStruct((2, R, TILE), BF16...]
    dot_general x6 -> x0, matrix products: 13.7 us -> none  [the longest x1 4.24 us: local(): jnp.einsum('ijab,iae->jbe', masked, factor_row, preferred_element_type=jn...]
  transfers between devices with their start and end apart: 5 -> 0, of which waited for: 5 -> 0; matrix products, arithmetic and copies ran while one was open for 1% -> 0% of each run, Pallas kernels for 0% -> 0%
where the time goes in v1:
time: 95.9 us; the launch traced here: 95.8 us
  Pallas kernels  91.6 us (96%)
  local copies, waits for them, and re-layouts  3.55 us (4%)
    pallas_call x1, Pallas kernels, local(): pl.pallas_call(kernel, out_shape=(jax.ShapeDtypeStruct((2, R, TILE), BF16...  91.6 us
    reshape x1, local copies, waits for them, and re-layouts, local(): inverse_adjoint = jnp.swapaxes(spread.reshape(2, TILE, TILE), 1, 2)  2.92 us

profile of v1, /device:TPU:1, one launch (start us, length us, event | category | flops | bytes accessed | tf_op | source)
XLA Modules:
  0.0 95.8 jit_solution(2587840871886961635)
XLA Ops:
  0.6 91.6 %shard_map.77 = (bf16[2,32,512]{2,1,0:T(8,128)(2,1)}, f32[2,16,4,8,512]{4,3,2,1,0:T(8,128)}) custom-call(bf16[2,32,512]{2,1,0:T(8,128)(2,1)} %panel.1, bf16[2,512,512]{2,1,0:T(8,128)(2,1)} %inverse.1, bf16[2,2,512,512]{3,2,1,0:T(8,128)(2,1)} %trail_hbm.1, bf16[2,32,512]{2,1,0:T(8,128)(2,1)} %factor_grad.1, s32[2,2]{1,0:T(2,128)} %present.1, s32[32]{0:T(128)} %supernode.1), custom_call_target="tpu_custom_call" | custom-call | tf_op jit(solution)/shard_map/pallas_call | solution.py:385
  92.3 0.0 copy-start
  92.3 2.9 %copy.8 = f32[2,512,512]{1,2,0:T(8,128)} copy(f32[2,512,512]{2,1,0:T(8,128)} %bitcast.3) | data formatting | bytes 4194304 | tf_op jit(solution)/shard_map/reshape | solution.py:422
  95.2 0.0 copy-done
  95.2 0.6 copy.10
Async XLA Ops:
  92.3 2.9 %copy-start = (bf16[2,32,512]{2,1,0:T(8,128)(2,1)S(1)}, bf16[2,32,512]{2,1,0:T(8,128)(2,1)}, u32[]{:S(2)}) copy-start(bf16[2,32,512]{2,1,0:T(8,128)(2,1)} %get-tuple-element.8) | copy-start | bytes 196612
